TPU v7x, 32 devices: a whole 2x2x4 slice. The times are simulated.
32 devices in a mesh: tok: 8 (over z, x), head: 4 (over y, core).
Axes of the slice: x: 2, y: 2, z: 4, core: 2. Of those that a mesh axis runs over, the one named last changes fastest.
Arguments:
- queries: bfloat16 [2048, 3072], P('tok', 'head'), may hold values from -96 to 96
- key_rows: bfloat16 [2048, 512], P('tok', 'head'), may hold values from -6 to 6
- value_rows: bfloat16 [2048, 512], P('tok', 'head'), may hold values from -12 to 12
- tile_mask: int32 [16, 16], P('tok'), may hold values from 0 to 1, as said below
- out_weight: bfloat16 [3072, 6144], P('head'), may hold values from -0.109375 to 0.109375
Outputs:
- mixed: bfloat16 [2048, 6144], P('tok', 'head')
Inputs may be any that keep to these rules, and one draw needn't show every extreme that they name: `tile_mask`: row r keeps key tile r; every row keeps between 1 and 8 tiles, and some row keeps exactly 8.
All inputs are finite; a program needn't handle non-finite values.
Results may differ from a plain program's by a relative error of at most 0.012.
Values may be sent and summed in bfloat16 or wider, within the bound.
A program may use at most 128 MiB of HBM per device.

v0:
```python
import math
import jax
import jax.numpy as jnp
from jax import lax
from jax.sharding import PartitionSpec as P

HD = 128
TILE = 128
NEGATIVE = -1e30
tiles_per_turn = 16


def tile_block(query_tile, key_chosen, value_chosen, shown_tiles, state, score_scale):
    scores = (
        jnp.einsum("qgjd,ckgd->gjqck", query_tile, key_chosen, preferred_element_type=jnp.float32)
        * score_scale
    )
    shown = shown_tiles[None, None, None, :]
    tile_max = jnp.where(shown, jnp.max(scores, axis=-1), NEGATIVE)
    prob_bf = jnp.where(shown[..., None], jnp.exp(scores - tile_max[..., None]), 0.0).astype(
        jnp.bfloat16
    )
    tile_sums = jnp.sum(prob_bf.astype(jnp.float32), axis=-1)
    tile_parts = jnp.einsum(
        "gjqck,ckgd->gjqcd", prob_bf, value_chosen, preferred_element_type=jnp.float32
    )
    running_max, denominator, numerator = state
    new_max = jnp.maximum(running_max, jnp.max(tile_max, axis=-1))
    rescale = jnp.exp(running_max - new_max)
    tile_weight = jnp.where(shown, jnp.exp(tile_max - new_max[..., None]), 0.0)
    denominator = denominator * rescale + jnp.sum(tile_weight * tile_sums, axis=-1)
    numerator = numerator * rescale[..., None] + jnp.sum(
        tile_weight[..., None] * tile_parts, axis=3
    )
    return (new_max, denominator, numerator)


def sweep_piece(state, query_tile, living, key_tiles, value_tiles, score_scale):
    tile_count = living.shape[0]
    block_tiles = min(tiles_per_turn, tile_count)
    ordering = jnp.argsort(1 - living, stable=True)
    live_total = jnp.sum(living)
    turn_count = (live_total + block_tiles - 1) // block_tiles

    def one_turn(turn_index, inner):
        offset = turn_index * block_tiles
        picked = lax.dynamic_slice_in_dim(ordering, offset, block_tiles)
        shown_tiles = offset + jnp.arange(block_tiles, dtype=jnp.int32) < live_total
        return tile_block(
            query_tile,
            jnp.take(key_tiles, picked, axis=0),
            jnp.take(value_tiles, picked, axis=0),
            shown_tiles,
            inner,
            score_scale,
        )

    return lax.fori_loop(0, turn_count, one_turn, state)


def per_device(queries, key_rows, value_rows, tile_mask, out_weight):
    own_rows = queries.shape[0]
    local_heads = queries.shape[1]
    slot_total = own_rows // TILE
    kv_local = key_rows.shape[1] // HD
    group_size = local_heads // HD // kv_local
    score_scale = 1.0 / math.sqrt(HD)
    query_tiles = queries.reshape(slot_total, TILE, kv_local, group_size, HD)
    slot_rows = [tile_mask[number] for number in range(slot_total)]
    slot_queries = [query_tiles[number] for number in range(slot_total)]
    slot_active = [jnp.int32(1) for number in range(slot_total)]
    empty_max = jnp.full((kv_local, group_size, TILE), NEGATIVE, jnp.float32)
    empty_sum = jnp.zeros((kv_local, group_size, TILE), jnp.float32)
    empty_out = jnp.zeros((kv_local, group_size, TILE, HD), jnp.float32)
    initial = tuple(((empty_max, empty_sum, empty_out) for number in range(len(slot_rows))))
    every_key, every_value = (
        lax.all_gather(key_rows, "tok", axis=0, tiled=True),
        lax.all_gather(value_rows, "tok", axis=0, tiled=True),
    )
    tile_count = every_key.shape[0] // TILE
    key_tiles = every_key.reshape(tile_count, TILE, kv_local, HD)
    value_tiles = every_value.reshape(tile_count, TILE, kv_local, HD)
    result = []
    for absorb_number in range(len(slot_rows)):
        living = slot_rows[absorb_number] * slot_active[absorb_number]
        result.append(
            sweep_piece(
                initial[absorb_number],
                slot_queries[absorb_number],
                living,
                key_tiles,
                value_tiles,
                score_scale,
            )
        )
    carries = tuple(result)
    finished = []
    for number in range(len(slot_rows)):
        running_max, denominator, numerator = carries[number]
        safe_sum = jnp.where(denominator > 0, denominator, 1.0)
        attended = numerator / safe_sum[..., None]
        finished.append(
            attended.transpose(2, 0, 1, 3).reshape(TILE, local_heads).astype(jnp.bfloat16)
        )
    own_stack = jnp.stack(finished[:slot_total])
    attention = own_stack.reshape(own_rows, local_heads)
    mixed = lax.psum_scatter(
        lax.dot_general(
            out_weight, attention, (((0,), (1,)), ((), ())), preferred_element_type=jnp.float32
        ).astype(jnp.bfloat16),
        "head",
        scatter_dimension=0,
        tiled=True,
    )
    return mixed.T


def solution(mesh):
    return jax.shard_map(
        per_device,
        mesh=mesh,
        in_specs=(
            P("tok", "head"),
            P("tok", "head"),
            P("tok", "head"),
            P("tok", None),
            P("head", None),
        ),
        out_specs=P("tok", "head"),
        check_vma=False,
    )
```

profile of v0, /device:TPU:0, one launch (start us, length us, event | category | flops | bytes accessed | tf_op | source)
XLA Modules:
  0.0 161.2 jit_solution(17541276726180953449)
XLA Ops:
  6.5 0.0 reduce-scatter.2.cloned.1.call-start
  6.5 1.4 subtract_bitcast_fusion.1
  8.6 1.3 sort.32
  10.5 1.3 sort.31
  11.9 33.3 %all_gather.7 = bf16[2048,128]{1,0:T(8,128)(2,1)S(1)} all-gather(bf16[256,128]{1,0:T(8,128)(2,1)} %param.13), channel_id=1, replica_groups=mesh['tok'=8,'head'=4] {'tok'}, dimensions={0}, use_global_device_ids=true | all-gather | bytes 589824 | tf_op jit(solution)/shard_map/all_gather | solution.py:78
  45.1 31.4 %all_gather.6 = bf16[2048,128]{1,0:T(8,128)(2,1)S(1)} all-gather(bf16[256,128]{1,0:T(8,128)(2,1)} %param.12), channel_id=1, replica_groups=mesh['tok'=8,'head'=4] {'tok'}, dimensions={0}, use_global_device_ids=true | all-gather | bytes 589824 | tf_op jit(solution)/shard_map/all_gather | solution.py:77
  76.5 0.6 gather_fusion.3
  77.2 0.6 gather_fusion.2
  77.9 0.6 gather_fusion.1
  78.5 0.6 gather_fusion
  79.2 1.1 fusion.37
  80.2 0.2 copy.32
  80.4 0.2 copy.22
  80.6 0.2 bitcast_select_fusion
  80.8 12.8 %while.33 = (s32[]{:T(128)}, f32[1,6,128]{2,1,0:T(8,128)S(1)}, f32[1,6,128]{2,1,0:T(8,128)S(1)}, f32[1,6,128,128]{3,2,1,0:T(8,128)S(1)}, s32[]{:T(128)}, /*index...) while((s32[]{:T(128)}, f32[1,6,128]{2,1,0:T(8,128)S(1)}, ...), condition=%wide.region_17.19_spmd, body=%wide.region_11.18_spmd.sunk | while | flops 827476224 | bytes 47396084 | solution.py:58
  80.8 3.6 %bitcast_reduce_fusion.5 = (f32[6,128,16]{1,0,2:T(8,128)S(1)}, f32[16,128,128,6]{2,1,3,0:T(8,128)}) fusion(bf16[128,1,6,128]{3,0,2,1:T(8,128)(2,1)S(1)} %get-tuple-element.525, bf16[16,128,1,128]{3,1,0,2:T(8,128)(2,1)S(1)} %get-tuple-element.524), kind=kOutput, calls=%fused_computation.32.clone.1 | convolution fusion | flops 405786624 | bytes 7061504 | tf_op jit(solution)/shard_map/while/body/qgjd,ckgd->gjqck/dot_general | solution.py:15
  84.5 0.0 copy-start
  84.5 0.8 add_compare_fusion.5
  85.3 0.1 fusion.57
  85.4 4.7 %convert_reduce_fusion.5 = f32[6,128,16]{1,0,2:T(8,128)S(1)} fusion(f32[6,128,16]{1,0,2:T(8,128)S(1)} %get-tuple-element.491, f32[16,128,128,6]{2,1,3,0:T(8,128)} %get-tuple-element.492, pred[16]{0:T(512)(128)(4,1)S(1)} %add_compare_fusion.5), kind=kLoop, calls=%fused_computation.36.clone.1 | loop fusion | flops 9424896 | bytes 6389776 | tf_op jit(solution)/shard_map/while/body/reduce_sum | solution.py:23
  90.1 0.1 multiply_reduce_fusion.5
  90.2 0.0 copy-done
  90.2 3.2 %fusion.59 = f32[6,128,128]{2,1,0:T(8,128)S(1)} fusion(f32[6,128,16]{1,0,2:T(8,128)S(1)} %get-tuple-element.494, bf16[16,128,1,128]{3,1,0,2:T(8,128)(2,1)S(1)} %get-tuple-element.526, f32[16,128,128,6]{2,1,3,0:T(8,128)S(1)} %copy-done, f32[6,128,16]{1,0,2:T(8,128)S(1)} %get-tuple-element.491, pred[16]{0:T(512)(128)(4,1)S(1)} %add_compare_fusion.5), kind=kOutput, calls=%fused_computation.30.clone.1 | convolution fusion | flops 411992064 | bytes 7307280 | tf_op jit(solution)/shard_map/while/body/gjqck,ckgd->gjqcd/dot_general | solution.py:24
  93.4 0.2 bitcast_add_fusion.11
  93.6 0.2 copy.23
  93.8 0.2 copy.31
  94.0 0.2 copy.19
  94.2 0.2 bitcast_select_fusion.2
  94.4 12.6 %while.32 = (s32[]{:T(128)}, f32[1,6,128]{2,1,0:T(8,128)S(1)}, f32[1,6,128]{2,1,0:T(8,128)S(1)}, f32[1,6,128,128]{3,2,1,0:T(8,128)S(1)}, s32[]{:T(128)}, /*index...) while((s32[]{:T(128)}, f32[1,6,128]{2,1,0:T(8,128)S(1)}, ...), condition=%wide.region_8.10_spmd, body=%wide.region_2.9_spmd.sunk | while | flops 827476224 | bytes 47396084 | solution.py:58
  94.4 3.6 %bitcast_reduce_fusion.4 = (f32[6,128,16]{1,0,2:T(8,128)S(1)}, f32[16,128,128,6]{2,1,3,0:T(8,128)}) fusion(bf16[128,1,6,128]{3,0,2,1:T(8,128)(2,1)S(1)} %get-tuple-element.558, bf16[16,128,1,128]{3,1,0,2:T(8,128)(2,1)S(1)} %get-tuple-element.557), kind=kOutput, calls=%fused_computation.7.clone.1 | convolution fusion | flops 405786624 | bytes 7061504 | tf_op jit(solution)/shard_map/while/body/qgjd,ckgd->gjqck/dot_general | solution.py:15
  98.1 0.0 copy-start.1
  98.1 0.7 add_compare_fusion.4
  98.8 0.1 fusion.52
  98.9 4.5 %convert_reduce_fusion.4 = f32[6,128,16]{1,0,2:T(8,128)S(1)} fusion(f32[6,128,16]{1,0,2:T(8,128)S(1)} %get-tuple-element.474, f32[16,128,128,6]{2,1,3,0:T(8,128)} %get-tuple-element.475, pred[16]{0:T(512)(128)(4,1)S(1)} %add_compare_fusion.4), kind=kLoop, calls=%fused_computation.11.clone.1 | loop fusion | flops 9424896 | bytes 6389776 | tf_op jit(solution)/shard_map/while/body/reduce_sum | solution.py:23
  103.4 0.1 multiply_reduce_fusion.4
  103.5 0.0 copy-done.1
  103.5 3.2 %fusion.54 = f32[6,128,128]{2,1,0:T(8,128)S(1)} fusion(f32[6,128,16]{1,0,2:T(8,128)S(1)} %get-tuple-element.477, bf16[16,128,1,128]{3,1,0,2:T(8,128)(2,1)S(1)} %get-tuple-element.559, f32[16,128,128,6]{2,1,3,0:T(8,128)S(1)} %copy-done.1, f32[6,128,16]{1,0,2:T(8,128)S(1)} %get-tuple-element.474, pred[16]{0:T(512)(128)(4,1)S(1)} %add_compare_fusion.4), kind=kOutput, calls=%fused_computation.5.clone.1 | convolution fusion | flops 411992064 | bytes 7307280 | tf_op jit(solution)/shard_map/while/body/gjqck,ckgd->gjqcd/dot_general | solution.py:24
  106.8 0.2 bitcast_add_fusion.9
  107.0 0.2 copy.20
  107.3 0.2 copy.24
  107.5 7.7 %fusion.32 = bf16[6144,256]{0,1:T(8,128)(2,1)} fusion(bf16[256,768]{1,0:T(8,128)(2,1)S(1)} %bitcast.214, bf16[768,6144]{1,0:T(8,128)(2,1)} %param.15), kind=kOutput, calls=%fused_computation.55 | convolution fusion | flops 2417491968 | bytes 12976128 | tf_op jit(solution)/shard_map/dot_general | solution.py:108
  115.2 0.0 reduce-scatter.2.cloned.1.call-update
  115.2 39.2 %reduce-scatter.2.cloned.1.call-done = bf16[1536,256]{0,1:T(8,128)(2,1)} async-done(((bf16[6144,256]{0,1:T(8,128)(2,1)}), bf16[1536,256]{0,1:T(8,128)(2,1)}) %reduce-scatter.2.cloned.1.call-update) | async-done | bytes 786448 | tf_op jit(solution)/shard_map/reduce_scatter | solution.py:107
  (25 shorter events, 0.3 us)
Async XLA Ops:
  6.5 147.9 %reduce-scatter.2.cloned.1.call-start = ((), (), s32[]{:S(2)}) async-start(), calls=%async_computation.1 | async-start | bytes 3932160 | tf_op jit(solution)/shard_map/reduce_scatter | solution.py:107
  84.5 5.7 %copy-start = (f32[16,128,128,6]{2,1,3,0:T(8,128)S(1)}, f32[16,128,128,6]{2,1,3,0:T(8,128)}, u32[]{:S(2)}) copy-start(f32[16,128,128,6]{2,1,3,0:T(8,128)} %get-tuple-element.492) | copy-start | bytes 18874372 | tf_op jit(solution)/shard_map/while
  98.1 5.4 %copy-start.1 = (f32[16,128,128,6]{2,1,3,0:T(8,128)S(1)}, f32[16,128,128,6]{2,1,3,0:T(8,128)}, u32[]{:S(2)}) copy-start(f32[16,128,128,6]{2,1,3,0:T(8,128)} %get-tuple-element.475) | copy-start | bytes 18874372 | tf_op jit(solution)/shard_map/while
Sparse Core Ops, SparseCore 0:
  115.3 39.0 reduce-scatter.1
where the time goes:
time: 161 us
  blocking collectives  64.7 us (40%)
  waiting for transfers between devices  39.2 us (24%)
  matrix products  21.4 us (13%)
  other arithmetic  16 us (10%)
  between operations  14.9 us (9%)
  local copies, waits for them, and re-layouts  4.9 us (3%)
    reduce_scatter x1, waiting for transfers between devices, per_device(): lax.psum_scatter(lax.dot_general(out_weight, attention, (((0,), (1,)), ((...  39.2 us
    all_gather x1, blocking collectives, per_device(): lax.all_gather(value_rows, 'tok', axis=0, tiled=True)  33.3 us
    all_gather x1, blocking collectives, per_device(): lax.all_gather(key_rows, 'tok', axis=0, tiled=True)  31.4 us
    reduce_sum x2, other arithmetic, tile_block(): tile_sums = jnp.sum(prob_bf.astype(jnp.float32), axis=-1)  9.13 us
    dot_general x1, matrix products, per_device(): lax.dot_general(out_weight, attention, (((0,), (1,)), ((), ())), preferre...  7.67 us
    dot_general x2, matrix products, tile_block(): jnp.einsum('qgjd,ckgd->gjqck', query_tile, key_chosen, preferred_element_...  7.29 us
    dot_general x2, matrix products, tile_block(): jnp.einsum('gjqck,ckgd->gjqcd', prob_bf, value_chosen, preferred_element_...  6.43 us
  transfers between devices with their start and end apart: 1, of which 1 were waited for; matrix products, arithmetic and copies ran while one was open for 0% of the time, Pallas kernels for 0%

commit v1 on v0

--- a/solution.py
+++ b/solution.py
@@ -75,7 +75,9 @@
     initial = tuple(((empty_max, empty_sum, empty_out) for number in range(len(slot_rows))))
     every_key, every_value = (
         lax.all_gather(key_rows, "tok", axis=0, tiled=True),
-        lax.all_gather(value_rows, "tok", axis=0, tiled=True),
+        jnp.concatenate(
+            lax.all_to_all(jnp.stack([value_rows] * lax.axis_size("tok")), "tok", 0, 0), axis=0
+        ),
     )
     tile_count = every_key.shape[0] // TILE
     key_tiles = every_key.reshape(tile_count, TILE, kv_local, HD)

time: 161 us -> 139 us (0.86)
  blocking collectives: 64.7 us -> 37.1 us
  starting transfers between devices: 0.01 us -> 7.32 us
  waiting for transfers between devices: 39.2 us -> 35.2 us
  local copies, waits for them, and re-layouts: 4.9 us -> 6.61 us
    all_gather x1 -> x0, blocking collectives: 33.3 us -> none  [per_device(): lax.all_gather(value_rows, 'tok', axis=0, tiled=True)]
    all_to_all x0 -> x1, starting transfers between devices: none -> 7.28 us  [per_device(): lax.all_to_all(jnp.stack([value_rows] * lax.axis_size('tok')), 'tok', 0, 0)]
    all_gather x1, blocking collectives: 31.4 us -> 37.1 us  [per_device(): lax.all_gather(key_rows, 'tok', axis=0, tiled=True)]
    reduce_scatter x1, waiting for transfers between devices: 39.2 us -> 35.2 us  [per_device(): lax.psum_scatter(lax.dot_general(out_weight, attention, (((0,), (1,)), ((...]
    another operation x2 -> x3, local copies, waits for them, and re-layouts: 0.01 us -> 1.7 us  [the longest x1 1.7 us: per_device(): jnp.stack([value_rows] * lax.axis_size('tok'))]
  transfers between devices with their start and end apart: 1 -> 2, of which waited for: 1 -> 1; matrix products, arithmetic and copies ran while one was open for 0% -> 5% of each run, Pallas kernels for 0% -> 0%
where the time goes in v1:
time: 139 us
  blocking collectives  37.1 us (27%)
  waiting for transfers between devices  35.2 us (25%)
  matrix products  21.4 us (15%)
  other arithmetic  15.9 us (11%)
  between operations  14.9 us (11%)
  starting transfers between devices  7.32 us (5%)
  local copies, waits for them, and re-layouts  6.61 us (5%)
    all_gather x1, blocking collectives, per_device(): lax.all_gather(key_rows, 'tok', axis=0, tiled=True)  37.1 us
    reduce_scatter x1, waiting for transfers between devices, per_device(): lax.psum_scatter(lax.dot_general(out_weight, attention, (((0,), (1,)), ((...  35.2 us
    reduce_sum x2, other arithmetic, tile_block(): tile_sums = jnp.sum(prob_bf.astype(jnp.float32), axis=-1)  9.13 us
    dot_general x1, matrix products, per_device(): lax.dot_general(out_weight, attention, (((0,), (1,)), ((), ())), preferre...  7.66 us
    dot_general x2, matrix products, tile_block(): jnp.einsum('qgjd,ckgd->gjqck', query_tile, key_chosen, preferred_element_...  7.3 us
    all_to_all x1, starting transfers between devices, per_device(): lax.all_to_all(jnp.stack([value_rows] * lax.axis_size('tok')), 'tok', 0, 0)  7.28 us
    dot_general x2, matrix products, tile_block(): jnp.einsum('gjqck,ckgd->gjqcd', prob_bf, value_chosen, preferred_element_...  6.43 us
  transfers between devices with their start and end apart: 2, of which 1 were waited for; matrix products, arithmetic and copies ran while one was open for 5% of the time, Pallas kernels for 0%

profile of v1, /device:TPU:0, one launch (start us, length us, event | category | flops | bytes accessed | tf_op | source)
XLA Modules:
  0.0 138.6 jit_solution(1998146545819599603)
XLA Ops:
  6.5 1.7 %stack.4 = bf16[8,256,128]{2,1,0:T(8,128)(2,1)} broadcast(bf16[256,128]{1,0:T(8,128)(2,1)} %param.13), dimensions={1,2} | broadcast | bytes 589824 | tf_op jit(solution)/shard_map/stack | solution.py:79
  8.2 7.3 %all-to-all-start = ((bf16[8,256,128]{2,1,0:T(8,128)(2,1)}), bf16[8,256,128]{2,1,0:T(8,128)(2,1)S(1)}, u32[]{:S(2)}, u32[]{:S(2)}) async-start(bf16[8,256,128]{2,1,0:T(8,128)(2,1)} %stack.4), calls=%async_computation | async-start | bytes 1048576 | tf_op jit(solution)/shard_map/all_to_all | solution.py:79
  15.5 0.0 reduce-scatter.2.cloned.1.call-start
  15.6 1.5 %subtract_bitcast_fusion.1 = (s32[16]{0:T(128)S(1)}, s32[16]{0:T(128)S(1)}, s32[]{:T(128)}, s32[]{:T(128)}) fusion(s32[2,16]{1,0:T(2,128)} %param.14), kind=kLoop, calls=%fused_computation.74 | loop fusion | flops 62 | bytes 264 | tf_op jit(solution)/shard_map/sub | solution.py:41
  17.0 37.1 %all_gather.3 = bf16[2048,128]{1,0:T(8,128)(2,1)S(1)} all-gather(bf16[256,128]{1,0:T(8,128)(2,1)} %param.12), channel_id=1, replica_groups=mesh['tok'=8,'head'=4] {'tok'}, dimensions={0}, use_global_device_ids=true | all-gather | bytes 589824 | tf_op jit(solution)/shard_map/all_gather | solution.py:77
  54.1 1.0 fusion.37
  55.2 1.3 sort.32
  57.7 0.2 copy.32
  57.9 0.2 copy.22
  58.1 0.6 gather_fusion.2
  58.8 1.3 sort.31
  60.1 0.6 gather_fusion
  60.7 0.2 copy.31
  60.9 0.2 copy.19
  61.1 0.0 all-to-all-done
  61.1 0.6 gather_fusion.3
  61.8 0.6 gather_fusion.1
  62.4 0.2 bitcast_select_fusion
  62.6 12.8 %while.33 = (s32[]{:T(128)}, f32[1,6,128]{2,1,0:T(8,128)S(1)}, f32[1,6,128]{2,1,0:T(8,128)S(1)}, f32[1,6,128,128]{3,2,1,0:T(8,128)S(1)}, s32[]{:T(128)}, /*index...) while((s32[]{:T(128)}, f32[1,6,128]{2,1,0:T(8,128)S(1)}, ...), condition=%wide.region_17.19_spmd, body=%wide.region_11.18_spmd.sunk | while | flops 827476224 | bytes 47396084 | solution.py:58
  62.7 3.6 %bitcast_reduce_fusion.5 = (f32[6,128,16]{1,0,2:T(8,128)S(1)}, f32[16,128,128,6]{2,1,3,0:T(8,128)}) fusion(bf16[128,1,6,128]{3,0,2,1:T(8,128)(2,1)S(1)} %get-tuple-element.525, bf16[16,128,1,128]{3,1,0,2:T(8,128)(2,1)S(1)} %get-tuple-element.524), kind=kOutput, calls=%fused_computation.32.clone.1 | convolution fusion | flops 405786624 | bytes 7061504 | tf_op jit(solution)/shard_map/while/body/qgjd,ckgd->gjqck/dot_general | solution.py:15
  66.3 0.0 copy-start
  66.3 0.8 add_compare_fusion.5
  67.1 0.1 fusion.57
  67.2 4.7 %convert_reduce_fusion.5 = f32[6,128,16]{1,0,2:T(8,128)S(1)} fusion(f32[6,128,16]{1,0,2:T(8,128)S(1)} %get-tuple-element.491, f32[16,128,128,6]{2,1,3,0:T(8,128)} %get-tuple-element.492, pred[16]{0:T(512)(128)(4,1)S(1)} %add_compare_fusion.5), kind=kLoop, calls=%fused_computation.36.clone.1 | loop fusion | flops 9424896 | bytes 6389776 | tf_op jit(solution)/shard_map/while/body/reduce_sum | solution.py:23
  71.9 0.1 multiply_reduce_fusion.5
  72.0 0.0 copy-done
  72.0 3.2 %fusion.59 = f32[6,128,128]{2,1,0:T(8,128)S(1)} fusion(f32[6,128,16]{1,0,2:T(8,128)S(1)} %get-tuple-element.494, bf16[16,128,1,128]{3,1,0,2:T(8,128)(2,1)S(1)} %get-tuple-element.526, f32[16,128,128,6]{2,1,3,0:T(8,128)S(1)} %copy-done, f32[6,128,16]{1,0,2:T(8,128)S(1)} %get-tuple-element.491, pred[16]{0:T(512)(128)(4,1)S(1)} %add_compare_fusion.5), kind=kOutput, calls=%fused_computation.30.clone.1 | convolution fusion | flops 411992064 | bytes 7307280 | tf_op jit(solution)/shard_map/while/body/gjqck,ckgd->gjqcd/dot_general | solution.py:24
  75.2 0.2 bitcast_add_fusion.11
  75.4 0.2 copy.23
  75.6 0.2 bitcast_select_fusion.2
  75.8 12.6 %while.32 = (s32[]{:T(128)}, f32[1,6,128]{2,1,0:T(8,128)S(1)}, f32[1,6,128]{2,1,0:T(8,128)S(1)}, f32[1,6,128,128]{3,2,1,0:T(8,128)S(1)}, s32[]{:T(128)}, /*index...) while((s32[]{:T(128)}, f32[1,6,128]{2,1,0:T(8,128)S(1)}, ...), condition=%wide.region_8.10_spmd, body=%wide.region_2.9_spmd.sunk | while | flops 827476224 | bytes 47396084 | solution.py:58
  75.9 3.7 %bitcast_reduce_fusion.4 = (f32[6,128,16]{1,0,2:T(8,128)S(1)}, f32[16,128,128,6]{2,1,3,0:T(8,128)}) fusion(bf16[128,1,6,128]{3,0,2,1:T(8,128)(2,1)S(1)} %get-tuple-element.558, bf16[16,128,1,128]{3,1,0,2:T(8,128)(2,1)S(1)} %get-tuple-element.557), kind=kOutput, calls=%fused_computation.7.clone.1 | convolution fusion | flops 405786624 | bytes 7061504 | tf_op jit(solution)/shard_map/while/body/qgjd,ckgd->gjqck/dot_general | solution.py:15
  79.5 0.0 copy-start.1
  79.5 0.7 add_compare_fusion.4
  80.3 0.1 fusion.52
  80.3 4.5 %convert_reduce_fusion.4 = f32[6,128,16]{1,0,2:T(8,128)S(1)} fusion(f32[6,128,16]{1,0,2:T(8,128)S(1)} %get-tuple-element.474, f32[16,128,128,6]{2,1,3,0:T(8,128)} %get-tuple-element.475, pred[16]{0:T(512)(128)(4,1)S(1)} %add_compare_fusion.4), kind=kLoop, calls=%fused_computation.11.clone.1 | loop fusion | flops 9424896 | bytes 6389776 | tf_op jit(solution)/shard_map/while/body/reduce_sum | solution.py:23
  84.8 0.1 multiply_reduce_fusion.4
  85.0 0.0 copy-done.1
  85.0 3.2 %fusion.54 = f32[6,128,128]{2,1,0:T(8,128)S(1)} fusion(f32[6,128,16]{1,0,2:T(8,128)S(1)} %get-tuple-element.477, bf16[16,128,1,128]{3,1,0,2:T(8,128)(2,1)S(1)} %get-tuple-element.559, f32[16,128,128,6]{2,1,3,0:T(8,128)S(1)} %copy-done.1, f32[6,128,16]{1,0,2:T(8,128)S(1)} %get-tuple-element.474, pred[16]{0:T(512)(128)(4,1)S(1)} %add_compare_fusion.4), kind=kOutput, calls=%fused_computation.5.clone.1 | convolution fusion | flops 411992064 | bytes 7307280 | tf_op jit(solution)/shard_map/while/body/gjqck,ckgd->gjqcd/dot_general | solution.py:24
  88.2 0.2 bitcast_add_fusion.9
  88.4 0.2 copy.20
  88.7 0.2 copy.24
  88.9 7.7 %fusion.32 = bf16[6144,256]{0,1:T(8,128)(2,1)} fusion(bf16[256,768]{1,0:T(8,128)(2,1)S(1)} %bitcast.214, bf16[768,6144]{1,0:T(8,128)(2,1)} %param.15), kind=kOutput, calls=%fused_computation.55 | convolution fusion | flops 2417491968 | bytes 12976128 | tf_op jit(solution)/shard_map/dot_general | solution.py:110
  96.6 0.0 reduce-scatter.2.cloned.1.call-update
  96.6 35.2 %reduce-scatter.2.cloned.1.call-done = bf16[1536,256]{0,1:T(8,128)(2,1)} async-done(((bf16[6144,256]{0,1:T(8,128)(2,1)}), bf16[1536,256]{0,1:T(8,128)(2,1)}) %reduce-scatter.2.cloned.1.call-update) | async-done | bytes 786448 | tf_op jit(solution)/shard_map/reduce_scatter | solution.py:109
  (25 shorter events, 0.3 us)
Async XLA Ops:
  8.2 52.9 %all-to-all-start = ((bf16[8,256,128]{2,1,0:T(8,128)(2,1)}), bf16[8,256,128]{2,1,0:T(8,128)(2,1)S(1)}, u32[]{:S(2)}, u32[]{:S(2)}) async-start(bf16[8,256,128]{2,1,0:T(8,128)(2,1)} %stack.4), calls=%async_computation | async-start | bytes 1048576 | tf_op jit(solution)/shard_map/all_to_all | solution.py:79
  15.5 116.3 %reduce-scatter.2.cloned.1.call-start = ((), (), s32[]{:S(2)}) async-start(), calls=%async_computation.2 | async-start | bytes 3932160 | tf_op jit(solution)/shard_map/reduce_scatter | solution.py:109
  66.3 5.7 %copy-start = (f32[16,128,128,6]{2,1,3,0:T(8,128)S(1)}, f32[16,128,128,6]{2,1,3,0:T(8,128)}, u32[]{:S(2)}) copy-start(f32[16,128,128,6]{2,1,3,0:T(8,128)} %get-tuple-element.492) | copy-start | bytes 18874372 | tf_op jit(solution)/shard_map/while
  79.5 5.4 %copy-start.1 = (f32[16,128,128,6]{2,1,3,0:T(8,128)S(1)}, f32[16,128,128,6]{2,1,3,0:T(8,128)}, u32[]{:S(2)}) copy-start(f32[16,128,128,6]{2,1,3,0:T(8,128)} %get-tuple-element.475) | copy-start | bytes 18874372 | tf_op jit(solution)/shard_map/while
Sparse Core Ops, SparseCore 0:
  96.7 35.0 reduce-scatter.1
